TPU v7x, 32 devices: a whole 2x2x4 slice. The times are simulated.
32 devices in a mesh: box: 2 (over core), row: 16 (over z, y, x).
Axes of the slice: x: 2, y: 2, z: 4, core: 2. Of those that a mesh axis runs over, the one named last changes fastest.
Arguments:
- dtn: float32 [4, 6, 384, 2304], P('box', None, 'row'), may hold values from -2 to 8, as said below
- interface_perm: int32 [2, 384], P('box'), may hold values from 0 to 383, each once within a row
Outputs:
- solution_first: float32 [2, 384, 3840], P('box', 'row')
- solution_second: float32 [2, 384, 6144], P('box', 'row')
- merged_map: float32 [2, 8, 384, 6144], P('box', None, 'row')
Inputs may be any that keep to these rules, and one draw needn't show every extreme that they name: `dtn`: each box's map, read as a (2304) x (2304) matrix, is symmetric and positive definite.
All inputs are finite; a program needn't handle non-finite values.
Results may differ from a plain program's by a relative error of at most 0.00012.
Values sent between devices are 32-bit elements; how exact they have to be, the bound alone decides.
A program may use at most 192 MiB of HBM per device.

v0:
```python
import jax
import jax.numpy as jnp
from jax import lax
from jax.sharding import PartitionSpec as P

F = 384


def partner(x, axis, stride):
    return lax.ppermute(x, axis, [(i, i ^ 1 << stride) for i in range(lax.axis_size(axis))])


def product(left, right):
    return jnp.dot(left, right, precision=lax.Precision.HIGHEST)


def block_factor(matrix):
    order = matrix.shape[0]
    block_size = 128
    count_blocks = order // block_size
    panels = []
    inverses = []
    for j in range(count_blocks):
        column = matrix[j * block_size :, j * block_size : (j + 1) * block_size]
        for k in range(j):
            offset = (j - k) * block_size
            column = column - product(panels[k][offset:], panels[k][offset : offset + block_size].T)
        diagonal_block = jnp.linalg.cholesky(column[:block_size])
        inverse = jax.scipy.linalg.solve_triangular(
            diagonal_block, jnp.eye(block_size, dtype=jnp.float32), lower=True
        )
        remainder = product(column[block_size:], inverse.T)
        panels.append(jnp.concatenate([diagonal_block, remainder], axis=0))
        inverses.append(inverse)
    return (panels, inverses, block_size)


def block_solve(factor, rhs):
    panels, inverses, block_size = factor
    count_blocks = len(panels)
    forward = []
    for j in range(count_blocks):
        residue = rhs[j * block_size : (j + 1) * block_size]
        for k in range(j):
            offset = (j - k) * block_size
            residue = residue - product(panels[k][offset : offset + block_size], forward[k])
        forward.append(product(inverses[j], residue))
    backward = [None] * count_blocks
    for j in reversed(range(count_blocks)):
        residue = forward[j]
        for k in range(j + 1, count_blocks):
            offset = (k - j) * block_size
            residue = residue - product(panels[j][offset : offset + block_size].T, backward[k])
        backward[j] = product(inverses[j].T, residue)
    return jnp.concatenate(backward, axis=0)


def slots(matrix, index, width):
    lead = matrix.shape[:-1]
    shaped = matrix.reshape(lead + (matrix.shape[-1] // width, width))
    taken = jnp.take(shaped, index, axis=len(lead))
    return taken.reshape(lead + (index.shape[0] * width,))


def body(dtn, interface_perm):
    first = dtn[0]
    second = dtn[1]
    count = first.shape[1]
    perm = interface_perm[0]
    shared_a, shared_b = (
        lax.all_gather(first[1], "row", axis=0, tiled=True),
        lax.all_gather(second[0], "row", axis=0, tiled=True),
    )
    block_bb = jnp.take(jnp.take(shared_b[:, :F], perm, axis=1), perm, axis=0)
    couple = shared_a[:, F : 2 * F] + block_bb
    outer_a = jnp.concatenate([first[0:1], first[2:6]], axis=0)
    outer_b = second[1:6]
    lift = jnp.concatenate(
        [outer_a[..., F : 2 * F], jnp.take(outer_b[..., :F], perm, axis=-1)], axis=0
    ).reshape(10 * count, F)
    factor = block_factor(couple)
    start = lax.axis_index("row") * count
    select = (
        jnp.arange(F, dtype=jnp.int32)[:, None]
        == start + jnp.arange(count, dtype=jnp.int32)[None, :]
    ).astype(jnp.float32)
    solved = block_solve(factor, jnp.concatenate([lift.T, select], axis=1)).T
    prod_a = product(solved, shared_a)
    placed = jnp.zeros_like(solved).at[:, perm].set(solved)
    prod_b = product(placed, shared_b)
    update = -jnp.concatenate([prod_a[:, :F], prod_a[:, 2 * F :], prod_b[:, F:]], axis=1)
    zero_block = jnp.zeros((5, count, 5 * F), jnp.float32)
    block_a = jnp.concatenate([outer_a[..., :F], outer_a[..., 2 * F :], zero_block], axis=-1)
    block_b = jnp.concatenate([zero_block, outer_b[..., F:]], axis=-1)
    merged = jnp.concatenate([block_a, block_b], axis=0) + update[: 10 * count].reshape(
        10, count, 10 * F
    )
    solution_first = update[10 * count :]
    half = lax.axis_index("box") % 2
    own_s = jnp.stack([2 - half, 7 - half])
    part_s = jnp.stack([1 + half, 6 + half])
    outer_p = jnp.array([0, 1, 3, 4, 5, 6, 8, 9], jnp.int32)
    outer_q = jnp.array([0, 2, 3, 4, 5, 7, 8, 9], jnp.int32)
    own_o = jnp.where(half == 0, outer_p, outer_q)
    part_o = jnp.where(half == 0, outer_q, outer_p)
    own_iface = jnp.take(merged, own_s, axis=0)
    own_outer = jnp.take(merged, own_o, axis=0).reshape(8 * count, 10 * F)
    full_own = lax.all_gather(own_iface, "row", axis=1, tiled=True)
    full_part = partner(full_own, "box", 0)
    own_rows = full_own.reshape(2 * F, 10 * F)
    part_rows = full_part.reshape(2 * F, 10 * F)
    couple_two = slots(own_rows, own_s, F) + slots(part_rows, part_s, F)
    lift_two = slots(own_outer, own_s, F)
    factor_two = block_factor(couple_two)
    select_two = (
        jnp.arange(2 * F, dtype=jnp.int32)[:, None]
        == half * F + start + jnp.arange(count, dtype=jnp.int32)[None, :]
    ).astype(jnp.float32)
    solved_two = block_solve(factor_two, jnp.concatenate([lift_two.T, select_two], axis=1)).T
    own_c = slots(product(solved_two, own_rows), own_o, F)
    part_c = slots(product(solved_two, part_rows), part_o, F)
    base = slots(own_outer, own_o, F) - own_c[: 8 * count]
    cross = -part_c[: 8 * count]
    left_cols = jnp.where(half == 0, base, cross)
    right_cols = jnp.where(half == 0, cross, base)
    merged_two = jnp.concatenate([left_cols, right_cols], axis=1).reshape(1, 8, count, 16 * F)
    sol_own = -own_c[8 * count :]
    sol_part = -part_c[8 * count :]
    sol_left = jnp.where(half == 0, sol_own, sol_part)
    sol_right = jnp.where(half == 0, sol_part, sol_own)
    solution_second = jnp.concatenate([sol_left, sol_right], axis=1)
    return (solution_first[None], solution_second[None], merged_two)


def solution(mesh):
    return jax.shard_map(
        body,
        mesh=mesh,
        in_specs=(P("box", None, "row", None), P("box", None)),
        out_specs=(P("box", "row", None), P("box", "row", None), P("box", None, "row", None)),
        check_vma=False,
    )
```

profile of v0, /device:TPU:1, one launch (start us, length us, event | category | flops | bytes accessed | tf_op | source)
XLA Modules:
  0.0 833.6 jit_solution(4822045302379656813)
XLA Ops:
  38.2 44.4 %all-gather.10.cloned.1.call-done = f32[1,1,384,2304]{3,1,0,2:T(1,128)} async-done(((f32[1,1,24,2304]{3,1,0,2:T(1,128)}), f32[1,1,384,2304]{3,1,0,2:T(1,128)}) %all-gather.10.cloned.1.call-update) | async-done | bytes 3538960 | tf_op jit(solution)/shard_map/all_gather | solution.py:72
  82.6 8.9 %copy.142 = f32[1,1,384,2304]{2,3,1,0:T(8,128)} copy(f32[1,1,384,2304]{3,1,0,2:T(1,128)} %all-gather.10.cloned.1.call-done) | data formatting | bytes 7077888 | tf_op jit(solution)/shard_map/all_gather | solution.py:72
  97.4 57.2 %all-gather.8.cloned.1.call-done = f32[1,1,384,2304]{3,1,0,2:T(1,128)} async-done(((f32[1,1,24,2304]{3,1,0,2:T(1,128)}), f32[1,1,384,2304]{3,1,0,2:T(1,128)}) %all-gather.8.cloned.1.call-update) | async-done | bytes 3538960 | tf_op jit(solution)/shard_map/all_gather | solution.py:71
  154.6 8.4 %copy.140 = f32[1,1,384,2304]{2,3,1,0:T(8,128)S(1)} copy(f32[1,1,384,2304]{3,1,0,2:T(1,128)} %all-gather.8.cloned.1.call-done) | data formatting | bytes 7077888 | tf_op jit(solution)/shard_map/all_gather | solution.py:71
  168.6 13.2 %cholesky.149 = f32[128,128]{1,0:T(8,128)} custom-call(f32[128,128]{1,0:T(8,128)} %fusion.91), custom_call_target="Cholesky" | custom-call | tf_op jit(solution)/shard_map/jit(cholesky)/cholesky | solution.py:28
  185.4 11.3 %custom-call.13 = f32[1,128,128]{1,2,0:T(8,128)} custom-call(f32[1,128,128]{2,1,0:T(8,128)} %fusion.61), custom_call_target="InvertDiagBlocksLowerTriangular" | custom-call | tf_op jit(solution)/shard_map/jit(_solve_triangular)/triangular_solve | solution.py:29
  211.2 13.2 %cholesky.160 = f32[128,128]{1,0:T(8,128)} custom-call(f32[128,128]{1,0:T(8,128)} %fusion.89), custom_call_target="Cholesky" | custom-call | tf_op jit(solution)/shard_map/jit(cholesky)/cholesky | solution.py:28
  228.6 11.3 %custom-call.14 = f32[1,128,128]{1,2,0:T(8,128)} custom-call(f32[1,128,128]{2,1,0:T(8,128)} %fusion.62), custom_call_target="InvertDiagBlocksLowerTriangular" | custom-call | tf_op jit(solution)/shard_map/jit(_solve_triangular)/triangular_solve | solution.py:29
  249.0 13.2 %cholesky.171 = f32[128,128]{1,0:T(8,128)} custom-call(f32[128,128]{1,0:T(8,128)} %fusion.87), custom_call_target="Cholesky" | custom-call | tf_op jit(solution)/shard_map/jit(cholesky)/cholesky | solution.py:28
  265.7 11.3 %custom-call.15 = f32[1,128,128]{1,2,0:T(8,128)} custom-call(f32[1,128,128]{2,1,0:T(8,128)} %fusion.63), custom_call_target="InvertDiagBlocksLowerTriangular" | custom-call | tf_op jit(solution)/shard_map/jit(_solve_triangular)/triangular_solve | solution.py:29
  293.7 9.5 %fusion.6 = f32[264,1920]{1,0:T(8,128)S(1)} fusion(f32[264,384]{0,1:T(8,128)S(1)} %scatter_custom_fusion, f32[384,2304]{0,1:T(8,128)} %bitcast.247), kind=kOutput, calls=%fused_computation.29 | convolution fusion | flops 2335703040 | bytes 5382144 | tf_op jit(solution)/shard_map/dot_general | solution.py:14
  313.0 143.2 %all-gather.6.cloned.1.call-done = f32[2,384,3840]{2,1,0:T(8,128)} async-done(((f32[2,24,3840]{2,1,0:T(8,128)}), f32[2,384,3840]{2,1,0:T(8,128)}) %all-gather.6.cloned.1.call-update) | async-done | bytes 11796496 | tf_op jit(solution)/shard_map/all_gather | solution.py:108
  490.6 14.9 %reshape.395 = f32[768,10,384]{2,1,0:T(8,128)} reshape(f32[2,384,3840]{2,1,0:T(8,128)} %all-gather.6.cloned.1.call-done) | data formatting | bytes 23592960 | tf_op jit(solution)/shard_map/reshape;reshape | solution.py:60
  505.5 14.5 %copy.156 = f32[768,10,384]{2,0,1:T(8,128)} copy(f32[768,10,384]{2,1,0:T(8,128)} %reshape.395) | data formatting | bytes 23592960 | tf_op jit(solution)/shard_map/reshape;reshape | solution.py:60
  520.0 12.4 %copy.183 = f32[768,3840]{0,1:T(8,128)} copy(f32[768,3840]{1,0:T(8,128)} %bitcast.241) | data formatting | bytes 23592960 | tf_op jit(solution)/shard_map/reshape | solution.py:110
  537.5 14.9 %reshape.396 = f32[768,10,384]{2,1,0:T(8,128)} reshape(f32[2,384,3840]{2,1,0:T(8,128)} %collective-permute-done) | data formatting | bytes 23592960 | tf_op jit(solution)/shard_map/reshape;reshape | solution.py:60
  552.4 14.5 %copy.158 = f32[768,10,384]{2,0,1:T(8,128)} copy(f32[768,10,384]{2,1,0:T(8,128)} %reshape.396) | data formatting | bytes 23592960 | tf_op jit(solution)/shard_map/reshape;reshape | solution.py:60
  579.1 11.7 %cholesky.182 = f32[128,128]{1,0:T(8,128)S(1)} custom-call(f32[128,128]{1,0:T(8,128)S(1)} %fusion.85), custom_call_target="Cholesky" | custom-call | tf_op jit(solution)/shard_map/jit(cholesky)/cholesky | solution.py:28
  592.1 9.8 %custom-call.16 = f32[1,128,128]{1,2,0:T(8,128)S(1)} custom-call(f32[1,128,128]{2,1,0:T(8,128)S(1)} %fusion.64), custom_call_target="InvertDiagBlocksLowerTriangular" | custom-call | tf_op jit(solution)/shard_map/jit(_solve_triangular)/triangular_solve | solution.py:29
  613.0 11.9 %cholesky.193 = f32[128,128]{1,0:T(8,128)S(1)} custom-call(f32[128,128]{1,0:T(8,128)S(1)} %fusion.83), custom_call_target="Cholesky" | custom-call | tf_op jit(solution)/shard_map/jit(cholesky)/cholesky | solution.py:28
  626.4 9.8 %custom-call.17 = f32[1,128,128]{1,2,0:T(8,128)S(1)} custom-call(f32[1,128,128]{2,1,0:T(8,128)S(1)} %fusion.65), custom_call_target="InvertDiagBlocksLowerTriangular" | custom-call | tf_op jit(solution)/shard_map/jit(_solve_triangular)/triangular_solve | solution.py:29
  640.8 11.7 %cholesky.204 = f32[128,128]{1,0:T(8,128)S(1)} custom-call(f32[128,128]{1,0:T(8,128)S(1)} %fusion.81), custom_call_target="Cholesky" | custom-call | tf_op jit(solution)/shard_map/jit(cholesky)/cholesky | solution.py:28
  653.9 9.8 %custom-call.18 = f32[1,128,128]{1,2,0:T(8,128)S(1)} custom-call(f32[1,128,128]{2,1,0:T(8,128)S(1)} %fusion.66), custom_call_target="InvertDiagBlocksLowerTriangular" | custom-call | tf_op jit(solution)/shard_map/jit(_solve_triangular)/triangular_solve | solution.py:29
  669.5 11.7 %cholesky.215 = f32[128,128]{1,0:T(8,128)S(1)} custom-call(f32[128,128]{1,0:T(8,128)S(1)} %fusion.79), custom_call_target="Cholesky" | custom-call | tf_op jit(solution)/shard_map/jit(cholesky)/cholesky | solution.py:28
  682.6 9.8 %custom-call.19 = f32[1,128,128]{1,2,0:T(8,128)S(1)} custom-call(f32[1,128,128]{2,1,0:T(8,128)S(1)} %fusion.67), custom_call_target="InvertDiagBlocksLowerTriangular" | custom-call | tf_op jit(solution)/shard_map/jit(_solve_triangular)/triangular_solve | solution.py:29
  695.5 11.9 %cholesky.226 = f32[128,128]{1,0:T(8,128)S(1)} custom-call(f32[128,128]{1,0:T(8,128)S(1)} %fusion.77), custom_call_target="Cholesky" | custom-call | tf_op jit(solution)/shard_map/jit(cholesky)/cholesky | solution.py:28
  708.7 9.8 %custom-call.20 = f32[1,128,128]{1,2,0:T(8,128)S(1)} custom-call(f32[1,128,128]{2,1,0:T(8,128)S(1)} %fusion.68), custom_call_target="InvertDiagBlocksLowerTriangular" | custom-call | tf_op jit(solution)/shard_map/jit(_solve_triangular)/triangular_solve | solution.py:29
  722.1 11.7 %cholesky.237 = f32[128,128]{1,0:T(8,128)S(1)} custom-call(f32[128,128]{1,0:T(8,128)S(1)} %fusion.75), custom_call_target="Cholesky" | custom-call | tf_op jit(solution)/shard_map/jit(cholesky)/cholesky | solution.py:28
  735.2 10.0 %custom-call.21 = f32[1,128,128]{1,2,0:T(8,128)S(1)} custom-call(f32[1,128,128]{2,1,0:T(8,128)S(1)} %fusion.69), custom_call_target="InvertDiagBlocksLowerTriangular" | custom-call | tf_op jit(solution)/shard_map/jit(_solve_triangular)/triangular_solve | solution.py:29
  754.2 12.4 %copy.184 = f32[768,3840]{0,1:T(8,128)} copy(f32[768,3840]{1,0:T(8,128)} %bitcast.56) | data formatting | bytes 23592960 | tf_op jit(solution)/shard_map/reshape | solution.py:111
  766.5 14.2 %fusion.8 = f32[216,10,384]{2,0,1:T(8,128)S(1)} fusion(f32[10,384,768]{2,1,0:T(8,128)} %bitcast.240, f32[768,216]{0,1:T(8,128)} %copy-done.9), kind=kOutput, calls=%fused_computation.101 | convolution fusion | flops 7644119040 | bytes 15777792 | tf_op jit(solution)/shard_map/dot_general | solution.py:14
  787.3 13.9 %fusion.10 = f32[216,10,384]{2,0,1:T(8,128)S(1)} fusion(f32[10,384,768]{2,1,0:T(8,128)} %bitcast.239, f32[768,216]{0,1:T(8,128)S(1)} %copy-done.10), kind=kOutput, calls=%fused_computation.103 | convolution fusion | flops 7644119040 | bytes 15777792 | tf_op jit(solution)/shard_map/dot_general | solution.py:14
  (300 shorter events, 231.5 us)
Async XLA Ops:
  7.2 75.4 %all-gather.10.cloned.1.call-start = ((), (), s32[]{:S(2)}) async-start(), calls=%async_computation.2 | async-start | bytes 3760128 | tf_op jit(solution)/shard_map/all_gather | solution.py:72
  8.4 27.4 %copy-start.12 = (f32[1,24,2304]{2,1,0:T(8,128)}, f32[1,24,2304]{2,1,0:T(8,128)S(1)}, u32[]{:S(2)}) copy-start(f32[1,24,2304]{2,1,0:T(8,128)S(1)} %get-tuple-element.19) | copy-start | bytes 663556
  9.4 145.2 %all-gather.8.cloned.1.call-start = ((), (), s32[]{:S(2)}) async-start(), calls=%async_computation.1 | async-start | bytes 3760128 | tf_op jit(solution)/shard_map/all_gather | solution.py:71
  10.3 445.9 %all-gather.6.cloned.1.call-start = ((), (), s32[]{:S(2)}) async-start(), calls=%async_computation | async-start | bytes 12533760 | tf_op jit(solution)/shard_map/all_gather | solution.py:108
  18.5 5.5 copy-start.25
  197.8 9.7 %copy-start.17 = (f32[128,128]{1,0:T(8,128)}, f32[128,128]{1,0:T(8,128)S(1)}, u32[]{:S(2)}) copy-start(f32[128,128]{1,0:T(8,128)S(1)} %fusion.36) | copy-start | bytes 196612
  199.2 6.6 copy-start.8
  200.4 7.1 copy-start.21
  201.8 5.7 copy-start.11
  242.2 2.0 copy-start.15
  276.9 8.4 %copy-start.18 = (f32[128,128]{1,0:T(8,128)S(1)}, f32[128,128]{1,0:T(8,128)}, u32[]{:S(2)}) copy-start(f32[128,128]{1,0:T(8,128)} %copy-done.17) | copy-start | bytes 196612
  293.7 9.5 %copy-start = (f32[264,1536]{1,0:T(8,128)S(1)}, f32[264,1536]{1,0:T(8,128)}, u32[]{:S(2)}) copy-start(f32[264,1536]{1,0:T(8,128)} %slice.410) | copy-start | bytes 4866052
  303.2 1.4 copy-start.7
  303.2 1.5 copy-start.13
  303.2 1.5 copy-start.20
  307.4 150.4 %copy-start.30 = (s32[8]{0:T(128)S(1)}, s32[8]{0:T(128)}, u32[]{:S(2)}) copy-start(s32[8]{0:T(128)} %constant.180.clone) | copy-start | bytes 100
  307.4 150.4 %copy-start.31 = (s32[8]{0:T(128)S(1)}, s32[8]{0:T(128)}, u32[]{:S(2)}) copy-start(s32[8]{0:T(128)} %constant.181.clone) | copy-start | bytes 100
  307.4 151.4 %copy-start.29 = (s32[2]{0:T(128)S(1)}, s32[2]{0:T(128)}, u32[]{:S(2)}) copy-start(s32[2]{0:T(128)} %get-tuple-element.14) | copy-start | bytes 28
  456.3 81.2 %collective-permute-start = (f32[2,384,3840]{2,1,0:T(8,128)}, f32[2,384,3840]{2,1,0:T(8,128)}, u32[]{:S(2)}, u32[]{:S(2)}) collective-permute-start(f32[2,384,3840]{2,1,0:T(8,128)} %all-gather.6.cloned.1.call-done), channel_id=1, source_target_pairs={{0,16},{16,0},{1,17},{17,1},{2,18},{18,2},{3,19},{19,3},{4,20},{20... | collective-permute-start | bytes 35389448 | tf_op jit(solution)/shard_map/ppermute | solution.py:10
  458.4 4.9 copy-start.26
  603.4 8.7 %copy-start.16 = (f32[640,128]{0,1:T(8,128)}, f32[640,128]{0,1:T(8,128)S(1)}, u32[]{:S(2)}) copy-start(f32[640,128]{0,1:T(8,128)S(1)} %convolution_subtract_fusion) | copy-start | bytes 983044
  638.0 55.1 %copy-start.24 = (f32[128,216]{0,1:T(8,128)S(1)}, f32[128,216]{0,1:T(8,128)}, u32[]{:S(2)}) copy-start(f32[128,216]{0,1:T(8,128)} %convolution_subtract_fusion.43) | copy-start | bytes 331780
  640.8 53.8 %copy-start.22 = (f32[256,128]{0,1:T(8,128)S(1)}, f32[256,128]{0,1:T(8,128)}, u32[]{:S(2)}) copy-start(f32[256,128]{0,1:T(8,128)} %convolution_subtract_fusion.15) | copy-start | bytes 393220
  669.0 50.1 %copy-start.23 = (f32[128,216]{0,1:T(8,128)S(1)}, f32[128,216]{0,1:T(8,128)}, u32[]{:S(2)}) copy-start(f32[128,216]{0,1:T(8,128)} %convolution_subtract_fusion.40) | copy-start | bytes 331780
  780.8 2.2 copy-start.28
  785.0 2.3 copy-start.1
  785.0 2.3 copy-start.10
  801.2 2.2 copy-start.27
  805.4 1.5 copy-start.2
  805.4 2.7 copy-start.3
  810.9 3.4 slice-start
  817.1 3.4 copy-start.4
  (5 other events, 5.0 us)
Sparse Core Ops, SparseCore 0:
  11.3 71.1 all-gather.9
  85.4 69.1 all-gather.7
  313.2 143.0 all-gather.5
where the time goes:
time: 843 us; the launch traced here: 834 us
  other arithmetic  262 us (31%)
  waiting for transfers between devices  245 us (29%)
  local copies, waits for them, and re-layouts  207 us (25%)
  matrix products  102 us (12%)
  between operations  15.8 us (2%)
    all_gather x1, waiting for transfers between devices, body(): full_own = lax.all_gather(own_iface, 'row', axis=1, tiled=True)  143 us
    another operation x27, other arithmetic, block_factor(): diagonal_block = jnp.linalg.cholesky(column[:block_size])  119 us
    another operation x18, other arithmetic, block_factor(): jax.scipy.linalg.solve_triangular(diagonal_block, jnp.eye(block_size, dty...  103 us
    dot_general x83, matrix products, product(): return jnp.dot(left, right, precision=lax.Precision.HIGHEST)  96.5 us
    another operation x4, local copies, waits for them, and re-layouts, slots(): shaped = matrix.reshape(lead + (matrix.shape[-1] // width, width))  58.8 us
    all_gather x1, waiting for transfers between devices, body(): lax.all_gather(first[1], 'row', axis=0, tiled=True)  57.2 us
    all_gather x1, waiting for transfers between devices, body(): lax.all_gather(second[0], 'row', axis=0, tiled=True)  44.4 us
    gather x9, local copies, waits for them, and re-layouts, slots(): taken = jnp.take(shaped, index, axis=len(lead))  30.8 us
  transfers between devices with their start and end apart: 4, of which 3 were waited for; matrix products, arithmetic and copies ran while one was open for 15% of the time, Pallas kernels for 0%

commit v1 on v0

--- a/solution.py
+++ b/solution.py
@@ -105,7 +105,12 @@
     part_o = jnp.where(half == 0, outer_q, outer_p)
     own_iface = jnp.take(merged, own_s, axis=0)
     own_outer = jnp.take(merged, own_o, axis=0).reshape(8 * count, 10 * F)
-    full_own = lax.all_gather(own_iface, "row", axis=1, tiled=True)
+    ring = [own_iface]
+    for hop in range(15):
+        ring.append(lax.ppermute(ring[-1], "row", [(dev, (dev + 1) % 16) for dev in range(16)]))
+    full_own = jnp.roll(
+        jnp.concatenate(ring[::-1], axis=1), (lax.axis_index("row") + 1) * ring[0].shape[1], axis=1
+    )
     full_part = partner(full_own, "box", 0)
     own_rows = full_own.reshape(2 * F, 10 * F)
     part_rows = full_part.reshape(2 * F, 10 * F)

time: 843 us -> 1030 us (1.22)
  waiting for transfers between devices: 245 us -> 366 us
  local copies, waits for them, and re-layouts: 207 us -> 260 us
  starting transfers between devices: 1.62 us -> 18.6 us
    ppermute x0 -> x15, waiting for transfers between devices: none -> 264 us  [body(): lax.ppermute(ring[-1], 'row', [(dev, (dev + 1) % 16) for dev in range(16)])]
    all_gather x1 -> x0, waiting for transfers between devices: 143 us -> none  [body(): full_own = lax.all_gather(own_iface, 'row', axis=1, tiled=True)]
    unnamed x72 -> x156, local copies, waits for them, and re-layouts: 18.7 us -> 62 us
    ppermute x1, starting transfers between devices: 1.49 us -> 17.1 us  [partner(): lax.ppermute(x, axis, [(i, i ^ 1 << stride) for i in range(lax.axis_size(...]
    reshape x1 -> x0, local copies, waits for them, and re-layouts: 12.4 us -> none  [body(): own_rows = full_own.reshape(2 * F, 10 * F)]
    dot_general x0 -> x1, local copies, waits for them, and re-layouts: none -> 12.4 us  [product(): return jnp.dot(left, right, precision=lax.Precision.HIGHEST)]
  transfers between devices with their start and end apart: 4 -> 18, of which waited for: 3 -> 17; matrix products, arithmetic and copies ran while one was open for 15% -> 12% of each run, Pallas kernels for 0% -> 0%
where the time goes in v1:
time: 1030 us; the launch traced here: 1020 us
  waiting for transfers between devices  366 us (36%)
  other arithmetic  263 us (26%)
  local copies, waits for them, and re-layouts  260 us (25%)
  matrix products  101 us (10%)
  starting transfers between devices  18.6 us (2%)
  between operations  16 us (2%)
    ppermute x15, waiting for transfers between devices, body(): lax.ppermute(ring[-1], 'row', [(dev, (dev + 1) % 16) for dev in range(16)])  264 us
    another operation x27, other arithmetic, block_factor(): diagonal_block = jnp.linalg.cholesky(column[:block_size])  119 us
    another operation x18, other arithmetic, block_factor(): jax.scipy.linalg.solve_triangular(diagonal_block, jnp.eye(block_size, dty...  103 us
    dot_general x83, matrix products, product(): return jnp.dot(left, right, precision=lax.Precision.HIGHEST)  95.5 us
    unnamed x156, local copies, waits for them, and re-layouts  62 us
    another operation x4, local copies, waits for them, and re-layouts, slots(): shaped = matrix.reshape(lead + (matrix.shape[-1] // width, width))  59 us
    all_gather x1, waiting for transfers between devices, body(): lax.all_gather(first[1], 'row', axis=0, tiled=True)  57.2 us
    all_gather x1, waiting for transfers between devices, body(): lax.all_gather(second[0], 'row', axis=0, tiled=True)  44.4 us
  transfers between devices with their start and end apart: 18, of which 17 were waited for; matrix products, arithmetic and copies ran while one was open for 12% of the time, Pallas kernels for 0%

profile of v1, /device:TPU:1, one launch (start us, length us, event | category | flops | bytes accessed | tf_op | source)
XLA Modules:
  0.0 1024.0 jit_solution(2195037046829804900)
XLA Ops:
  38.2 44.4 %all-gather.7.cloned.1.call-done = f32[1,1,384,2304]{3,1,0,2:T(1,128)} async-done(((f32[1,1,24,2304]{3,1,0,2:T(1,128)}), f32[1,1,384,2304]{3,1,0,2:T(1,128)}) %all-gather.7.cloned.1.call-update) | async-done | bytes 3538960 | tf_op jit(solution)/shard_map/all_gather | solution.py:72
  97.3 57.2 %all-gather.5.cloned.1.call-done = f32[1,1,384,2304]{3,1,0,2:T(1,128)} async-done(((f32[1,1,24,2304]{3,1,0,2:T(1,128)}), f32[1,1,384,2304]{3,1,0,2:T(1,128)}) %all-gather.5.cloned.1.call-update) | async-done | bytes 3538960 | tf_op jit(solution)/shard_map/all_gather | solution.py:71
  168.8 13.2 %cholesky.149 = f32[128,128]{1,0:T(8,128)} custom-call(f32[128,128]{1,0:T(8,128)} %fusion.91), custom_call_target="Cholesky" | custom-call | tf_op jit(solution)/shard_map/jit(cholesky)/cholesky | solution.py:28
  211.4 13.2 %cholesky.160 = f32[128,128]{1,0:T(8,128)} custom-call(f32[128,128]{1,0:T(8,128)} %fusion.89), custom_call_target="Cholesky" | custom-call | tf_op jit(solution)/shard_map/jit(cholesky)/cholesky | solution.py:28
  248.8 13.2 %cholesky.171 = f32[128,128]{1,0:T(8,128)} custom-call(f32[128,128]{1,0:T(8,128)} %fusion.87), custom_call_target="Cholesky" | custom-call | tf_op jit(solution)/shard_map/jit(cholesky)/cholesky | solution.py:28
  312.5 18.3 %collective-permute-done = f32[2,24,3840]{2,1,0:T(8,128)S(1)} collective-permute-done((f32[2,24,3840]{2,1,0:T(8,128)S(1)}, f32[2,24,3840]{2,1,0:T(8,128)S(1)}, u32[]{:S(2)}, u32[]{:S(2)}) %collective-permute-start) | collective-permute-done | bytes 737312 | tf_op jit(solution)/shard_map/ppermute | solution.py:110
  331.7 18.6 %collective-permute-done.1 = f32[2,24,3840]{2,1,0:T(8,128)S(1)} collective-permute-done((f32[2,24,3840]{2,1,0:T(8,128)S(1)}, f32[2,24,3840]{2,1,0:T(8,128)S(1)}, u32[]{:S(2)}, u32[]{:S(2)}) %collective-permute-start.1) | collective-permute-done | bytes 737312 | tf_op jit(solution)/shard_map/ppermute | solution.py:110
  351.2 17.7 %collective-permute-done.2 = f32[2,24,3840]{2,1,0:T(8,128)S(1)} collective-permute-done((f32[2,24,3840]{2,1,0:T(8,128)S(1)}, f32[2,24,3840]{2,1,0:T(8,128)S(1)}, u32[]{:S(2)}, u32[]{:S(2)}) %collective-permute-start.2) | collective-permute-done | bytes 737312 | tf_op jit(solution)/shard_map/ppermute | solution.py:110
  369.8 16.9 %collective-permute-done.3 = f32[2,24,3840]{2,1,0:T(8,128)S(1)} collective-permute-done((f32[2,24,3840]{2,1,0:T(8,128)S(1)}, f32[2,24,3840]{2,1,0:T(8,128)S(1)}, u32[]{:S(2)}, u32[]{:S(2)}) %collective-permute-start.3) | collective-permute-done | bytes 737312 | tf_op jit(solution)/shard_map/ppermute | solution.py:110
  387.5 16.0 %collective-permute-done.4 = f32[2,24,3840]{2,1,0:T(8,128)S(1)} collective-permute-done((f32[2,24,3840]{2,1,0:T(8,128)S(1)}, f32[2,24,3840]{2,1,0:T(8,128)S(1)}, u32[]{:S(2)}, u32[]{:S(2)}) %collective-permute-start.4) | collective-permute-done | bytes 737312 | tf_op jit(solution)/shard_map/ppermute | solution.py:110
  404.5 15.2 %collective-permute-done.5 = f32[2,24,3840]{2,1,0:T(8,128)S(1)} collective-permute-done((f32[2,24,3840]{2,1,0:T(8,128)S(1)}, f32[2,24,3840]{2,1,0:T(8,128)S(1)}, u32[]{:S(2)}, u32[]{:S(2)}) %collective-permute-start.5) | collective-permute-done | bytes 737312 | tf_op jit(solution)/shard_map/ppermute | solution.py:110
  420.6 14.3 %collective-permute-done.6 = f32[2,24,3840]{2,1,0:T(8,128)S(1)} collective-permute-done((f32[2,24,3840]{2,1,0:T(8,128)S(1)}, f32[2,24,3840]{2,1,0:T(8,128)S(1)}, u32[]{:S(2)}, u32[]{:S(2)}) %collective-permute-start.6) | collective-permute-done | bytes 737312 | tf_op jit(solution)/shard_map/ppermute | solution.py:110
  435.8 14.5 %collective-permute-done.7 = f32[2,24,3840]{2,1,0:T(8,128)S(1)} collective-permute-done((f32[2,24,3840]{2,1,0:T(8,128)S(1)}, f32[2,24,3840]{2,1,0:T(8,128)S(1)}, u32[]{:S(2)}, u32[]{:S(2)}) %collective-permute-start.7) | collective-permute-done | bytes 737312 | tf_op jit(solution)/shard_map/ppermute | solution.py:110
  451.1 15.6 %collective-permute-done.8 = f32[2,24,3840]{2,1,0:T(8,128)S(1)} collective-permute-done((f32[2,24,3840]{2,1,0:T(8,128)S(1)}, f32[2,24,3840]{2,1,0:T(8,128)S(1)}, u32[]{:S(2)}, u32[]{:S(2)}) %collective-permute-start.8) | collective-permute-done | bytes 737312 | tf_op jit(solution)/shard_map/ppermute | solution.py:110
  467.7 16.8 %collective-permute-done.9 = f32[2,24,3840]{2,1,0:T(8,128)S(1)} collective-permute-done((f32[2,24,3840]{2,1,0:T(8,128)S(1)}, f32[2,24,3840]{2,1,0:T(8,128)S(1)}, u32[]{:S(2)}, u32[]{:S(2)}) %collective-permute-start.9) | collective-permute-done | bytes 737312 | tf_op jit(solution)/shard_map/ppermute | solution.py:110
  485.4 18.0 %collective-permute-done.10 = f32[2,24,3840]{2,1,0:T(8,128)S(1)} collective-permute-done((f32[2,24,3840]{2,1,0:T(8,128)S(1)}, f32[2,24,3840]{2,1,0:T(8,128)S(1)}, u32[]{:S(2)}, u32[]{:S(2)}) %collective-permute-start.10) | collective-permute-done | bytes 737312 | tf_op jit(solution)/shard_map/ppermute | solution.py:110
  504.2 19.1 %collective-permute-done.11 = f32[2,24,3840]{2,1,0:T(8,128)S(1)} collective-permute-done((f32[2,24,3840]{2,1,0:T(8,128)S(1)}, f32[2,24,3840]{2,1,0:T(8,128)S(1)}, u32[]{:S(2)}, u32[]{:S(2)}) %collective-permute-start.11) | collective-permute-done | bytes 737312 | tf_op jit(solution)/shard_map/ppermute | solution.py:110
  524.1 20.3 %collective-permute-done.12 = f32[2,24,3840]{2,1,0:T(8,128)S(1)} collective-permute-done((f32[2,24,3840]{2,1,0:T(8,128)S(1)}, f32[2,24,3840]{2,1,0:T(8,128)S(1)}, u32[]{:S(2)}, u32[]{:S(2)}) %collective-permute-start.12) | collective-permute-done | bytes 737312 | tf_op jit(solution)/shard_map/ppermute | solution.py:110
  545.4 21.4 %collective-permute-done.13 = f32[2,24,3840]{2,1,0:T(8,128)} collective-permute-done((f32[2,24,3840]{2,1,0:T(8,128)S(1)}, f32[2,24,3840]{2,1,0:T(8,128)}, u32[]{:S(2)}, u32[]{:S(2)}) %collective-permute-start.13) | collective-permute-done | bytes 737312 | tf_op jit(solution)/shard_map/ppermute | solution.py:110
  567.0 21.2 %collective-permute-done.14 = f32[2,24,3840]{2,1,0:T(8,128)} collective-permute-done((f32[2,24,3840]{2,1,0:T(8,128)}, f32[2,24,3840]{2,1,0:T(8,128)}, u32[]{:S(2)}, u32[]{:S(2)}) %collective-permute-start.14) | collective-permute-done | bytes 737312 | tf_op jit(solution)/shard_map/ppermute | solution.py:110
  633.7 17.1 %collective-permute-start.15 = (f32[2,384,3840]{2,1,0:T(8,128)}, f32[2,384,3840]{2,1,0:T(8,128)}, u32[]{:S(2)}, u32[]{:S(2)}) collective-permute-start(f32[2,384,3840]{2,1,0:T(8,128)} %constant_dynamic-slice_fusion), channel_id=1, source_target_pairs={{0,16},{16,0},{1,17},{17,1},{2,18},{18,2},{3,19},{19,3},{4,20},{20... | collective-permute-start | bytes 35389448 | tf_op jit(solution)/shard_map/ppermute | solution.py:10
  683.6 14.9 %reshape.395 = f32[768,10,384]{2,1,0:T(8,128)} reshape(f32[2,384,3840]{2,1,0:T(8,128)} %constant_dynamic-slice_fusion) | data formatting | bytes 23592960 | tf_op jit(solution)/shard_map/reshape;reshape | solution.py:60
  698.5 14.4 %copy.157 = f32[768,10,384]{2,0,1:T(8,128)} copy(f32[768,10,384]{2,1,0:T(8,128)} %reshape.395) | data formatting | bytes 23592960 | tf_op jit(solution)/shard_map/reshape;reshape | solution.py:60
  712.9 12.4 %copy.184 = f32[3840,768]{1,0:T(8,128)} copy(f32[3840,768]{0,1:T(8,128)} %bitcast.239) | data formatting | bytes 23592960 | tf_op jit(solution)/shard_map/dot_general | solution.py:14
  730.4 15.2 %reshape.396 = f32[768,10,384]{2,1,0:T(8,128)} reshape(f32[2,384,3840]{2,1,0:T(8,128)} %collective-permute-done.15) | data formatting | bytes 23592960 | tf_op jit(solution)/shard_map/reshape;reshape | solution.py:60
  745.7 14.5 %copy.159 = f32[768,10,384]{2,0,1:T(8,128)} copy(f32[768,10,384]{2,1,0:T(8,128)} %reshape.396) | data formatting | bytes 23592960 | tf_op jit(solution)/shard_map/reshape;reshape | solution.py:60
  772.1 11.7 %cholesky.182 = f32[128,128]{1,0:T(8,128)S(1)} custom-call(f32[128,128]{1,0:T(8,128)S(1)} %fusion.85), custom_call_target="Cholesky" | custom-call | tf_op jit(solution)/shard_map/jit(cholesky)/cholesky | solution.py:28
  806.2 11.9 %cholesky.193 = f32[128,128]{1,0:T(8,128)S(1)} custom-call(f32[128,128]{1,0:T(8,128)S(1)} %fusion.83), custom_call_target="Cholesky" | custom-call | tf_op jit(solution)/shard_map/jit(cholesky)/cholesky | solution.py:28
  886.5 12.1 %cholesky.226 = f32[128,128]{1,0:T(8,128)S(1)} custom-call(f32[128,128]{1,0:T(8,128)S(1)} %fusion.77), custom_call_target="Cholesky" | custom-call | tf_op jit(solution)/shard_map/jit(cholesky)/cholesky | solution.py:28
  945.4 12.4 %copy.185 = f32[768,3840]{0,1:T(8,128)} copy(f32[768,3840]{1,0:T(8,128)} %bitcast.56) | data formatting | bytes 23592960 | tf_op jit(solution)/shard_map/reshape | solution.py:116
  957.7 14.0 %fusion.8 = f32[216,10,384]{2,0,1:T(8,128)S(1)} fusion(f32[10,384,768]{2,1,0:T(8,128)} %bitcast.241, f32[768,216]{0,1:T(8,128)} %copy-done.9), kind=kOutput, calls=%fused_computation.101 | convolution fusion | flops 7644119040 | bytes 15777792 | tf_op jit(solution)/shard_map/dot_general | solution.py:14
  978.3 14.0 %fusion.10 = f32[216,10,384]{2,0,1:T(8,128)S(1)} fusion(f32[10,384,768]{2,1,0:T(8,128)} %bitcast.240, f32[768,216]{0,1:T(8,128)S(1)} %copy-done.10), kind=kOutput, calls=%fused_computation.103 | convolution fusion | flops 7644119040 | bytes 15777792 | tf_op jit(solution)/shard_map/dot_general | solution.py:14
  (414 shorter events, 438.5 us)
Async XLA Ops:
  7.2 75.4 %all-gather.7.cloned.1.call-start = ((), (), s32[]{:S(2)}) async-start(), calls=%async_computation.1 | async-start | bytes 3760128 | tf_op jit(solution)/shard_map/all_gather | solution.py:72
  8.4 27.3 %copy-start.38 = (f32[1,24,2304]{2,1,0:T(8,128)}, f32[1,24,2304]{2,1,0:T(8,128)S(1)}, u32[]{:S(2)}) copy-start(f32[1,24,2304]{2,1,0:T(8,128)S(1)} %get-tuple-element.19) | copy-start | bytes 663556
  9.4 145.2 %all-gather.5.cloned.1.call-start = ((), (), s32[]{:S(2)}) async-start(), calls=%async_computation | async-start | bytes 3760128 | tf_op jit(solution)/shard_map/all_gather | solution.py:71
  198.1 9.6 copy-start.43
  292.5 11.8 %copy-start.6 = (f32[264,384]{1,0:T(8,128)}, f32[264,384]{1,0:T(8,128)S(1)}, u32[]{:S(2)}) copy-start(f32[264,384]{1,0:T(8,128)S(1)} %slice.409) | copy-start | bytes 1216516
  311.3 19.5 %collective-permute-start = (f32[2,24,3840]{2,1,0:T(8,128)S(1)}, f32[2,24,3840]{2,1,0:T(8,128)S(1)}, u32[]{:S(2)}, u32[]{:S(2)}) collective-permute-start(f32[2,24,3840]{2,1,0:T(8,128)S(1)} %broadcast_select_fusion.2), channel_id=1, source_target_pairs={{0,1},{1,2},{2,3},{3,4},{4,5},{5,6},{6,7},{7,8},{8,9},{9,10},{10,1... | collective-permute-start | bytes 2211848 | tf_op jit(solution)/shard_map/ppermute | solution.py:110
  331.7 18.6 %collective-permute-start.1 = (f32[2,24,3840]{2,1,0:T(8,128)S(1)}, f32[2,24,3840]{2,1,0:T(8,128)S(1)}, u32[]{:S(2)}, u32[]{:S(2)}) collective-permute-start(f32[2,24,3840]{2,1,0:T(8,128)S(1)} %collective-permute-done), channel_id=1, source_target_pairs={{0,1},{1,2},{2,3},{3,4},{4,5},{5,6},{6,7},{7,8},{8,9},{9,10},{10,1... | collective-permute-start | bytes 2211848 | tf_op jit(solution)/shard_map/ppermute | solution.py:110
  351.2 17.7 %collective-permute-start.2 = (f32[2,24,3840]{2,1,0:T(8,128)S(1)}, f32[2,24,3840]{2,1,0:T(8,128)S(1)}, u32[]{:S(2)}, u32[]{:S(2)}) collective-permute-start(f32[2,24,3840]{2,1,0:T(8,128)S(1)} %collective-permute-done.1), channel_id=1, source_target_pairs={{0,1},{1,2},{2,3},{3,4},{4,5},{5,6},{6,7},{7,8},{8,9},{9,10},{10,1... | collective-permute-start | bytes 2211848 | tf_op jit(solution)/shard_map/ppermute | solution.py:110
  369.8 16.9 %collective-permute-start.3 = (f32[2,24,3840]{2,1,0:T(8,128)S(1)}, f32[2,24,3840]{2,1,0:T(8,128)S(1)}, u32[]{:S(2)}, u32[]{:S(2)}) collective-permute-start(f32[2,24,3840]{2,1,0:T(8,128)S(1)} %collective-permute-done.2), channel_id=1, source_target_pairs={{0,1},{1,2},{2,3},{3,4},{4,5},{5,6},{6,7},{7,8},{8,9},{9,10},{10,1... | collective-permute-start | bytes 2211848 | tf_op jit(solution)/shard_map/ppermute | solution.py:110
  387.5 16.0 %collective-permute-start.4 = (f32[2,24,3840]{2,1,0:T(8,128)S(1)}, f32[2,24,3840]{2,1,0:T(8,128)S(1)}, u32[]{:S(2)}, u32[]{:S(2)}) collective-permute-start(f32[2,24,3840]{2,1,0:T(8,128)S(1)} %collective-permute-done.3), channel_id=1, source_target_pairs={{0,1},{1,2},{2,3},{3,4},{4,5},{5,6},{6,7},{7,8},{8,9},{9,10},{10,1... | collective-permute-start | bytes 2211848 | tf_op jit(solution)/shard_map/ppermute | solution.py:110
  404.5 15.2 %collective-permute-start.5 = (f32[2,24,3840]{2,1,0:T(8,128)S(1)}, f32[2,24,3840]{2,1,0:T(8,128)S(1)}, u32[]{:S(2)}, u32[]{:S(2)}) collective-permute-start(f32[2,24,3840]{2,1,0:T(8,128)S(1)} %collective-permute-done.4), channel_id=1, source_target_pairs={{0,1},{1,2},{2,3},{3,4},{4,5},{5,6},{6,7},{7,8},{8,9},{9,10},{10,1... | collective-permute-start | bytes 2211848 | tf_op jit(solution)/shard_map/ppermute | solution.py:110
  420.6 14.3 %collective-permute-start.6 = (f32[2,24,3840]{2,1,0:T(8,128)S(1)}, f32[2,24,3840]{2,1,0:T(8,128)S(1)}, u32[]{:S(2)}, u32[]{:S(2)}) collective-permute-start(f32[2,24,3840]{2,1,0:T(8,128)S(1)} %collective-permute-done.5), channel_id=1, source_target_pairs={{0,1},{1,2},{2,3},{3,4},{4,5},{5,6},{6,7},{7,8},{8,9},{9,10},{10,1... | collective-permute-start | bytes 2211848 | tf_op jit(solution)/shard_map/ppermute | solution.py:110
  435.8 14.5 %collective-permute-start.7 = (f32[2,24,3840]{2,1,0:T(8,128)S(1)}, f32[2,24,3840]{2,1,0:T(8,128)S(1)}, u32[]{:S(2)}, u32[]{:S(2)}) collective-permute-start(f32[2,24,3840]{2,1,0:T(8,128)S(1)} %collective-permute-done.6), channel_id=1, source_target_pairs={{0,1},{1,2},{2,3},{3,4},{4,5},{5,6},{6,7},{7,8},{8,9},{9,10},{10,1... | collective-permute-start | bytes 2211848 | tf_op jit(solution)/shard_map/ppermute | solution.py:110
  451.1 15.7 %collective-permute-start.8 = (f32[2,24,3840]{2,1,0:T(8,128)S(1)}, f32[2,24,3840]{2,1,0:T(8,128)S(1)}, u32[]{:S(2)}, u32[]{:S(2)}) collective-permute-start(f32[2,24,3840]{2,1,0:T(8,128)S(1)} %collective-permute-done.7), channel_id=1, source_target_pairs={{0,1},{1,2},{2,3},{3,4},{4,5},{5,6},{6,7},{7,8},{8,9},{9,10},{10,1... | collective-permute-start | bytes 2211848 | tf_op jit(solution)/shard_map/ppermute | solution.py:110
  467.7 16.8 %collective-permute-start.9 = (f32[2,24,3840]{2,1,0:T(8,128)S(1)}, f32[2,24,3840]{2,1,0:T(8,128)S(1)}, u32[]{:S(2)}, u32[]{:S(2)}) collective-permute-start(f32[2,24,3840]{2,1,0:T(8,128)S(1)} %collective-permute-done.8), channel_id=1, source_target_pairs={{0,1},{1,2},{2,3},{3,4},{4,5},{5,6},{6,7},{7,8},{8,9},{9,10},{10,1... | collective-permute-start | bytes 2211848 | tf_op jit(solution)/shard_map/ppermute | solution.py:110
  485.3 18.0 %collective-permute-start.10 = (f32[2,24,3840]{2,1,0:T(8,128)S(1)}, f32[2,24,3840]{2,1,0:T(8,128)S(1)}, u32[]{:S(2)}, u32[]{:S(2)}) collective-permute-start(f32[2,24,3840]{2,1,0:T(8,128)S(1)} %collective-permute-done.9), channel_id=1, source_target_pairs={{0,1},{1,2},{2,3},{3,4},{4,5},{5,6},{6,7},{7,8},{8,9},{9,10},{10,1... | collective-permute-start | bytes 2211848 | tf_op jit(solution)/shard_map/ppermute | solution.py:110
  504.2 19.1 %collective-permute-start.11 = (f32[2,24,3840]{2,1,0:T(8,128)S(1)}, f32[2,24,3840]{2,1,0:T(8,128)S(1)}, u32[]{:S(2)}, u32[]{:S(2)}) collective-permute-start(f32[2,24,3840]{2,1,0:T(8,128)S(1)} %collective-permute-done.10), channel_id=1, source_target_pairs={{0,1},{1,2},{2,3},{3,4},{4,5},{5,6},{6,7},{7,8},{8,9},{9,10},{10,1... | collective-permute-start | bytes 2211848 | tf_op jit(solution)/shard_map/ppermute | solution.py:110
  524.1 20.3 %collective-permute-start.12 = (f32[2,24,3840]{2,1,0:T(8,128)S(1)}, f32[2,24,3840]{2,1,0:T(8,128)S(1)}, u32[]{:S(2)}, u32[]{:S(2)}) collective-permute-start(f32[2,24,3840]{2,1,0:T(8,128)S(1)} %collective-permute-done.11), channel_id=1, source_target_pairs={{0,1},{1,2},{2,3},{3,4},{4,5},{5,6},{6,7},{7,8},{8,9},{9,10},{10,1... | collective-permute-start | bytes 2211848 | tf_op jit(solution)/shard_map/ppermute | solution.py:110
  545.3 21.4 %collective-permute-start.13 = (f32[2,24,3840]{2,1,0:T(8,128)S(1)}, f32[2,24,3840]{2,1,0:T(8,128)}, u32[]{:S(2)}, u32[]{:S(2)}) collective-permute-start(f32[2,24,3840]{2,1,0:T(8,128)S(1)} %collective-permute-done.12), channel_id=1, source_target_pairs={{0,1},{1,2},{2,3},{3,4},{4,5},{5,6},{6,7},{7,8},{8,9},{9,10},{10,1... | collective-permute-start | bytes 2211848 | tf_op jit(solution)/shard_map/ppermute | solution.py:110
  566.8 21.4 %collective-permute-start.14 = (f32[2,24,3840]{2,1,0:T(8,128)}, f32[2,24,3840]{2,1,0:T(8,128)}, u32[]{:S(2)}, u32[]{:S(2)}) collective-permute-start(f32[2,24,3840]{2,1,0:T(8,128)} %collective-permute-done.13), channel_id=1, source_target_pairs={{0,1},{1,2},{2,3},{3,4},{4,5},{5,6},{6,7},{7,8},{8,9},{9,10},{10,1... | collective-permute-start | bytes 2211848 | tf_op jit(solution)/shard_map/ppermute | solution.py:110
  567.0 27.5 %copy-start.34 = (f32[2,24,3840]{2,1,0:T(8,128)S(1)}, f32[2,24,3840]{2,1,0:T(8,128)}, u32[]{:S(2)}) copy-start(f32[2,24,3840]{2,1,0:T(8,128)} %copy-done.33) | copy-start | bytes 2211844
  567.0 28.4 %copy-start.32 = (f32[2,24,3840]{2,1,0:T(8,128)S(1)}, f32[2,24,3840]{2,1,0:T(8,128)}, u32[]{:S(2)}) copy-start(f32[2,24,3840]{2,1,0:T(8,128)} %copy-done.31) | copy-start | bytes 2211844
  567.0 29.4 %copy-start.30 = (f32[2,24,3840]{2,1,0:T(8,128)S(1)}, f32[2,24,3840]{2,1,0:T(8,128)}, u32[]{:S(2)}) copy-start(f32[2,24,3840]{2,1,0:T(8,128)} %copy-done.29) | copy-start | bytes 2211844
  624.0 26.8 %copy-start.57 = (s32[8]{0:T(128)S(1)}, s32[8]{0:T(128)}, u32[]{:S(2)}) copy-start(s32[8]{0:T(128)} %constant.197.clone) | copy-start | bytes 100
  624.0 26.8 %copy-start.58 = (s32[8]{0:T(128)S(1)}, s32[8]{0:T(128)}, u32[]{:S(2)}) copy-start(s32[8]{0:T(128)} %constant.198.clone) | copy-start | bytes 100
  624.0 27.8 %copy-start.56 = (s32[2]{0:T(128)S(1)}, s32[2]{0:T(128)}, u32[]{:S(2)}) copy-start(s32[2]{0:T(128)} %get-tuple-element.14) | copy-start | bytes 28
  633.7 96.7 %collective-permute-start.15 = (f32[2,384,3840]{2,1,0:T(8,128)}, f32[2,384,3840]{2,1,0:T(8,128)}, u32[]{:S(2)}, u32[]{:S(2)}) collective-permute-start(f32[2,384,3840]{2,1,0:T(8,128)} %constant_dynamic-slice_fusion), channel_id=1, source_target_pairs={{0,16},{16,0},{1,17},{17,1},{2,18},{18,2},{3,19},{19,3},{4,20},{20... | collective-permute-start | bytes 35389448 | tf_op jit(solution)/shard_map/ppermute | solution.py:10
  805.1 53.8 %copy-start.51 = (f32[128,216]{0,1:T(8,128)S(1)}, f32[128,216]{0,1:T(8,128)}, u32[]{:S(2)}) copy-start(f32[128,216]{0,1:T(8,128)} %convolution_subtract_fusion.45) | copy-start | bytes 331780
  805.1 54.5 %copy-start.47 = (f32[384,128]{0,1:T(8,128)S(1)}, f32[384,128]{0,1:T(8,128)}, u32[]{:S(2)}) copy-start(f32[384,128]{0,1:T(8,128)} %convolution_subtract_fusion.5) | copy-start | bytes 589828
  805.2 79.0 %copy-start.50 = (f32[128,216]{0,1:T(8,128)S(1)}, f32[128,216]{0,1:T(8,128)}, u32[]{:S(2)}) copy-start(f32[128,216]{0,1:T(8,128)} %convolution_subtract_fusion.43) | copy-start | bytes 331780
  831.0 54.6 %copy-start.48 = (f32[256,128]{0,1:T(8,128)S(1)}, f32[256,128]{0,1:T(8,128)}, u32[]{:S(2)}) copy-start(f32[256,128]{0,1:T(8,128)} %convolution_subtract_fusion.15) | copy-start | bytes 393220
  857.6 52.8 %copy-start.49 = (f32[128,216]{0,1:T(8,128)S(1)}, f32[128,216]{0,1:T(8,128)}, u32[]{:S(2)}) copy-start(f32[128,216]{0,1:T(8,128)} %convolution_subtract_fusion.40) | copy-start | bytes 331780
  (45 other events, 129.8 us)
Sparse Core Ops, SparseCore 0:
  11.3 71.1 all-gather.6
  85.3 69.1 all-gather.4
